TPU v7x, 32 devices: a whole 2x2x4 slice. The times are simulated.
32 devices in a mesh: row: 4 (over x, core), col: 8 (over z, y).
Axes of the slice: x: 2, y: 2, z: 4, core: 2. Of those that a mesh axis runs over, the one named last changes fastest.
Arguments:
- vectors: float32 [32768, 128], P(('col', 'row')), may hold values from -6 to 6
- tile_values: bfloat16 [4, 8, 22, 512, 512], P('row', 'col'), may hold values from 0 to 1
- tile_rows: int32 [4, 8, 22], P('row', 'col'), may hold values from 0 to 15, as said below
- tile_cols: int32 [4, 8, 22], P('row', 'col'), may hold values from 0 to 7
- tile_count: int32 [4, 8], P('row', 'col'), may hold values from 1 to 22, as said below
- degrees: int32 [32768], replicated, may hold values from 16 to 255
Outputs:
- result: float32 [32768, 128], P(('row', 'col'))
Inputs may be any that keep to these rules, and one draw needn't show every extreme that they name: `tile_rows`: within one device no two slots name the same pair of tile row and tile column. `tile_count`: some device has all 22 slots live.
All inputs are finite; a program needn't handle non-finite values.
Results may differ from a plain program's by a relative error of at most 0.0003.
Values sent between devices are 32-bit elements; how exact they have to be, the bound alone decides.
A program may use at most 128 MiB of HBM per device.

v0:
```python
import jax
import jax.numpy as jnp
from jax import lax
from jax.sharding import PartitionSpec as P


def body(vectors, tile_values, tile_rows, tile_cols, tile_count, degrees):
    row_count = lax.axis_size("row")
    col_count = lax.axis_size("col")
    row_index = lax.axis_index("row")
    col_index = lax.axis_index("col")
    piece_rows = vectors.shape[0]
    vec_width = vectors.shape[1]
    tile_side = tile_values.shape[-1]
    slot_count = tile_values.shape[2]
    col_tiles = piece_rows * row_count // tile_side
    row_tiles = piece_rows * col_count // tile_side
    inv_root = lax.rsqrt(degrees.astype(jnp.float32))
    own_start = (col_index * row_count + row_index) * piece_rows
    own_scale = lax.dynamic_slice_in_dim(inv_root, own_start, piece_rows)
    own_piece = vectors * own_scale[:, None]
    gathered = lax.all_gather(own_piece, "row", axis=0, tiled=True)
    row_ids = tile_rows[0, 0]
    col_ids = tile_cols[0, 0]
    live_mask = (jnp.arange(slot_count, dtype=jnp.int32) < tile_count[0, 0]).astype(jnp.float32)
    col_pick = (col_ids[:, None] == jnp.arange(col_tiles, dtype=jnp.int32)[None, :]).astype(
        jnp.float32
    )
    chosen = jnp.dot(
        col_pick,
        gathered.reshape(col_tiles, tile_side * vec_width),
        precision=lax.Precision.HIGHEST,
        preferred_element_type=jnp.float32,
    )
    chosen = chosen.reshape(slot_count, tile_side, vec_width)
    contrib = jnp.einsum(
        "kij,kjv->kiv",
        tile_values[0, 0],
        chosen,
        precision=lax.Precision.HIGHEST,
        preferred_element_type=jnp.float32,
    )
    contrib = contrib.reshape(slot_count, tile_side * vec_width)
    row_pick = (row_ids[:, None] == jnp.arange(row_tiles, dtype=jnp.int32)[None, :]).astype(
        jnp.float32
    ) * live_mask[:, None]
    out_start = (row_index * col_count + col_index) * piece_rows
    out_scale = lax.dynamic_slice_in_dim(inv_root, out_start, piece_rows)
    partial_value = jnp.dot(
        row_pick.T, contrib, precision=lax.Precision.HIGHEST, preferred_element_type=jnp.float32
    )
    partial_value = partial_value.reshape(row_tiles * tile_side, vec_width)
    result_rows = lax.psum_scatter(partial_value, "col", scatter_dimension=0, tiled=True)
    return result_rows * out_scale[:, None]


def solution(mesh):
    placed = (
        P(("col", "row"), None),
        P("row", "col", None, None, None),
        P("row", "col", None),
        P("row", "col", None),
        P("row", "col"),
        P(),
    )
    return jax.shard_map(
        body, mesh=mesh, in_specs=placed, out_specs=P(("row", "col"), None), check_vma=False
    )
```

profile of v0, /device:TPU:0, one launch (start us, length us, event | category | flops | bytes accessed | tf_op | source)
XLA Modules:
  0.0 182.7 jit_solution(7455030561679033844)
XLA Ops:
  6.5 0.0 all-gather.2.cloned.1.call-start
  6.5 0.9 convert_rsqrt_fusion
  7.5 2.0 %broadcast_multiply_fusion.1 = f32[1024,128]{1,0:T(8,128)} fusion(f32[1024,128]{1,0:T(8,128)} %param.6, f32[1024]{0:T(1024)S(1)} %get-tuple-element.6), kind=kLoop, calls=%fused_computation.7 | loop fusion | flops 131072 | bytes 1052672 | tf_op jit(solution)/shard_map/mul | solution.py:21
  9.5 0.0 all-gather.2.cloned.1.call-update
  9.6 0.0 reduce-scatter.2.cloned.1.call-start
  10.3 24.7 %all-gather.2.cloned.1.call-done = f32[4096,128]{1,0:T(8,128)} async-done(((f32[1024,128]{1,0:T(8,128)}), f32[4096,128]{1,0:T(8,128)}) %all-gather.2.cloned.1.call-update) | async-done | bytes 2097168 | tf_op jit(solution)/shard_map/all_gather | solution.py:22
  35.0 2.0 %reshape.20 = f32[8,65536]{1,0:T(8,128)S(1)} reshape(f32[4096,128]{1,0:T(8,128)} %all-gather.2.cloned.1.call-done) | data formatting | bytes 4194304 | tf_op jit(solution)/shard_map/reshape | solution.py:31
  37.0 5.2 %fusion.8 = f32[22,512,128]{2,0,1:T(8,128)} fusion(f32[8,65536]{1,0:T(8,128)S(1)} %reshape.20, s32[22]{0:T(128)} %bitcast.25), kind=kOutput, calls=%fused_computation.4 | convolution fusion | flops 138412208 | bytes 7864408 | tf_op jit(solution)/shard_map/dot_general | solution.py:29
  42.2 20.3 %fusion.3 = f32[22,512,128]{1,2,0:T(8,128)} fusion(bf16[1,1,22,512,512]{4,3,2,1,0:T(8,128)(2,1)} %param.7, f32[22,512,128]{2,0,1:T(8,128)} %fusion.8), kind=kOutput, calls=%fused_computation.3 | convolution fusion | flops 8858370048 | bytes 23068672 | tf_op jit(solution)/shard_map/kij,kjv->kiv/dot_general | solution.py:36
  62.5 6.3 %copy.7 = f32[22,512,128]{2,1,0:T(8,128)} copy(f32[22,512,128]{1,2,0:T(8,128)} %fusion.3) | data formatting | bytes 11534336 | tf_op jit(solution)/shard_map/kij,kjv->kiv/dot_general | solution.py:36
  68.7 3.3 %pad = f32[24,512,128]{2,1,0:T(8,128)S(1)} pad(f32[22,512,128]{2,1,0:T(8,128)} %copy.7, f32[]{:T(128)} %constant.4.clone.1), padding=0_2x0_0x0_0 | pad | bytes 12058628
  72.1 0.0 copy-start
  72.1 3.6 %copy.9 = f32[3,8,512,128]{3,1,2,0:T(8,128)S(1)} copy(f32[3,8,512,128]{3,2,1,0:T(8,128)S(1)} %bitcast.23) | data formatting | bytes 12582912
  75.7 0.0 copy-done
  75.7 5.8 %fusion.10 = f32[16,65536]{1,0:T(8,128)} fusion(f32[22,65536]{1,0:T(8,128)S(1)} %bitcast.24, f32[22]{0:T(128)S(1)} %compare_convert_fusion, s32[22]{0:T(128)S(1)} %bitcast.26), kind=kOutput, calls=%fused_computation.10 | convolution fusion | flops 276824768 | bytes 9961648 | tf_op jit(solution)/shard_map/dot_general | solution.py:49
  81.5 3.8 %reshape.22 = f32[8192,128]{1,0:T(8,128)} reshape(f32[16,65536]{1,0:T(8,128)} %fusion.10) | data formatting | bytes 8388608 | tf_op jit(solution)/shard_map/reshape | solution.py:52
  85.3 0.0 reduce-scatter.2.cloned.1.call-update
  85.3 88.5 %reduce-scatter.2.cloned.1.call-done = f32[1024,128]{1,0:T(8,128)} async-done(((f32[8192,128]{1,0:T(8,128)}), f32[1024,128]{1,0:T(8,128)}) %reduce-scatter.2.cloned.1.call-update) | async-done | bytes 524304 | tf_op jit(solution)/shard_map/reduce_scatter | solution.py:53
  173.8 2.0 %broadcast_multiply_fusion = f32[1024,128]{1,0:T(8,128)} fusion(f32[1024,128]{1,0:T(8,128)} %reduce-scatter.2.cloned.1.call-done, f32[1024]{0:T(1024)S(1)} %get-tuple-element.5), kind=kLoop, calls=%fused_computation.6 | loop fusion | flops 131072 | bytes 1052672 | tf_op jit(solution)/shard_map/mul | solution.py:54
  (2 shorter events, 0.0 us)
Async XLA Ops:
  6.5 28.5 %all-gather.2.cloned.1.call-start = ((), (), s32[]{:S(2)}) async-start(), calls=%async_computation.1 | async-start | bytes 2621440 | tf_op jit(solution)/shard_map/all_gather | solution.py:22
  9.6 164.3 %reduce-scatter.2.cloned.1.call-start = ((), (), s32[]{:S(2)}) async-start(), calls=%async_computation.2 | async-start | bytes 4718592 | tf_op jit(solution)/shard_map/reduce_scatter | solution.py:53
  72.1 3.7 %copy-start = (s32[1,1,22]{2,1,0:T(1,128)S(1)}, s32[1,1,22]{2,1,0:T(1,128)}, u32[]{:S(2)}) copy-start(s32[1,1,22]{2,1,0:T(1,128)} %param.8) | copy-start | bytes 268
Sparse Core Ops, SparseCore 0:
  9.7 25.2 all-gather.1
  85.5 88.3 reduce-scatter.1
where the time goes:
time: 183 us
  waiting for transfers between devices  113 us (62%)
  matrix products  31.3 us (17%)
  local copies, waits for them, and re-layouts  19 us (10%)
  between operations  14.1 us (8%)
  other arithmetic  5.01 us (3%)
    reduce_scatter x1, waiting for transfers between devices, body(): lax.psum_scatter(partial_value, 'col', scatter_dimension=0, tiled=True)  88.5 us
    all_gather x1, waiting for transfers between devices, body(): gathered = lax.all_gather(own_piece, 'row', axis=0, tiled=True)  24.7 us
    dot_general x1, matrix products, body(): jnp.einsum('kij,kjv->kiv', tile_values[0, 0], chosen, precision=lax.Preci...  20.3 us
    unnamed x4, local copies, waits for them, and re-layouts  6.95 us
    dot_general x1, local copies, waits for them, and re-layouts, body(): jnp.einsum('kij,kjv->kiv', tile_values[0, 0], chosen, precision=lax.Preci...  6.26 us
    dot_general x1, matrix products, body(): jnp.dot(row_pick.T, contrib, precision=lax.Precision.HIGHEST, preferred_e...  5.75 us
    dot_general x1, matrix products, body(): jnp.dot(col_pick, gathered.reshape(col_tiles, tile_side * vec_width), pre...  5.23 us
    reshape x1, local copies, waits for them, and re-layouts, body(): partial_value = partial_value.reshape(row_tiles * tile_side, vec_width)  3.83 us
  transfers between devices with their start and end apart: 2, of which 2 were waited for; matrix products, arithmetic and copies ran while one was open for 0% of the time, Pallas kernels for 0%

commit v1 on v0

v1 whole, which is shorter than its diff:
```python
import functools

import jax
import jax.numpy as jnp
from jax import lax
from jax.experimental import pallas as pl
from jax.experimental.pallas import tpu as pltpu
from jax.sharding import PartitionSpec as P

MESH = pl.DeviceIdType.MESH


def inner_size(col_count):
    inner = 1
    while inner * inner * 4 <= col_count and col_count % (inner * 2) == 0:
        inner *= 2
    return inner


def kernel(
    dims,
    rows_s, cols_s, count_s, vec_ref, deg_ref, tiles_hbm, out_ref,
    tiles_v, gath, split_v, sums, inb, outb, prev_s, last_s,
    tile_sem, d_send, d_recv, m_send, m_recv, f_send, f_recv,
    i_send, i_recv, o_send, o_recv,
):
    R, A, B, piece, width, side, slots = dims
    C = A * B
    tpp = piece // side
    chips = R // 2
    me_row = lax.axis_index("row")
    me_col = lax.axis_index("col")
    chip, core = me_row // 2, me_row % 2
    mate = chip * 2 + (1 - core)
    a, b = me_col // B, me_col % B
    lanes = 128

    tile_copy = pltpu.make_async_copy(tiles_hbm.at[0, 0], tiles_v, tile_sem)
    tile_copy.start()

    def rdma(src, dst, ssem, rsem, where):
        return pltpu.make_async_remote_copy(
            src_ref=src, dst_ref=dst, send_sem=ssem, recv_sem=rsem,
            device_id=where, device_id_type=MESH,
        )

    barrier = pltpu.get_barrier_semaphore()

    def greet(where):
        pl.semaphore_signal(barrier, inc=1, device_id=where, device_id_type=MESH)

    greet({"row": mate})
    for j in range(1, chips):
        greet({"row": lax.rem(chip + j, chips) * 2 + core})
    conds = []
    if B > 1:
        conds += [(b > 0, me_col - 1), (b < B - 1, me_col + 1)]
    if A > 1:
        conds += [(a > 0, me_col - B), (a < A - 1, me_col + B)]
    for cond, other in conds:
        @pl.when(cond)
        def _(other=other):
            greet({"col": other})
    peers = jnp.int32(chips)
    for cond, other in conds:
        peers = peers + jnp.where(cond, 1, 0)
    pl.semaphore_wait(barrier, peers)

    def part(c):
        return pl.ds(c * side, side)

    directs, mates, forwards = {}, [], {}
    for c in range(tpp):
        for j in range(1, chips):
            dst = lax.rem(chip + j, chips) * 2 + core
            cp = rdma(vec_ref.at[part(c)], gath.at[me_row, part(c)],
                      d_send.at[j - 1, c], d_recv.at[j - 1, c], {"row": dst})
            cp.start()
            directs[j, c] = cp
    for c in range(tpp):
        cp = rdma(vec_ref.at[part(c)], gath.at[me_row, part(c)],
                  m_send.at[c], m_recv.at[c], {"row": mate})
        cp.start()
        mates.append(cp)

    count = count_s[0, 0]

    def link(k, _):
        rk = rows_s[0, 0, k]
        v = jnp.int32(slots)
        for j in range(slots):
            v = jnp.where((rows_s[0, 0, j] == rk) & (j < k), j, v)
        prev_s[k] = v
        return 0

    lax.fori_loop(0, slots, link, 0)

    def ends(r, _):
        v = jnp.int32(slots)
        for j in range(slots):
            v = jnp.where((rows_s[0, 0, j] == r) & (j < count), j, v)
        last_s[r] = v
        return 0

    lax.fori_loop(0, C * tpp, ends, 0)
    sums[slots] = jnp.zeros((side, width), jnp.float32)

    def factors(first):
        d = deg_ref[pl.ds(first, 1), :].astype(jnp.float32)
        return jnp.broadcast_to(lax.rsqrt(d), (lanes, lanes)).T

    col_first = me_col * (R * piece // lanes)

    def scale(get, r, c):
        def step(q, _):
            f = factors(col_first + (r * piece + c * side) // lanes + q)
            x = get(pl.ds(c * side + q * lanes, lanes)) * f
            hi = x.astype(jnp.bfloat16)
            lo = (x - hi.astype(jnp.float32)).astype(jnp.bfloat16)
            at = pl.ds(pl.multiple_of(q * lanes, lanes), lanes)
            split_v[r * tpp + c, at, :width] = hi
            split_v[r * tpp + c, at, width:] = lo
            return 0

        lax.fori_loop(0, side // lanes, step, 0)

    def landed(r, c, ssem, rsem):
        rdma(gath.at[r, part(c)], gath.at[r, part(c)], ssem, rsem, {"row": mate}).wait_recv()

    for c in range(tpp):
        scale(lambda s: vec_ref[s, :], me_row, c)
    for c in range(tpp):
        landed(mate, c, m_send.at[c], m_recv.at[c])
        scale(lambda s: gath[mate, s, :], mate, c)
    for c in range(tpp):
        for j in range(1, chips):
            src = lax.rem(chip - j + chips, chips) * 2 + core
            landed(src, c, d_send.at[j - 1, c], d_recv.at[j - 1, c])
            cp = rdma(gath.at[src, part(c)], gath.at[src, part(c)],
                      f_send.at[j - 1, c], f_recv.at[j - 1, c], {"row": mate})
            cp.start()
            forwards[j, c] = cp
            scale(lambda s, src=src: gath[src, s, :], src, c)
    for c in range(tpp):
        for j in range(1, chips):
            src = lax.rem(chip - j + chips, chips) * 2 + (1 - core)
            landed(src, c, f_send.at[j - 1, c], f_recv.at[j - 1, c])
            scale(lambda s, src=src: gath[src, s, :], src, c)

    tile_copy.wait()

    def product(k, _):
        both = jnp.dot(tiles_v[k], split_v[cols_s[0, 0, k]], preferred_element_type=jnp.float32)
        sums[k] = both[:, :width] + both[:, width:] + sums[prev_s[k]]
        return 0

    lax.fori_loop(0, slots, product, 0)

    order = sorted_table(A)

    def pick(s):
        v = jnp.int32(order[0][s])
        for i in range(1, A):
            v = jnp.where(a == i, order[i][s], v)
        return v

    def own(d, t, u):
        return sums[last_s[(d * B + t) * tpp + u]]

    def inner_steps(action):
        for s in range(A):
            d = pick(s)
            for dist in range(B - 1, 0, -1):
                for right in (True, False):
                    t = b + dist if right else b - dist
                    slot = t + 1 if right else t
                    to = me_col + 1 if right else me_col - 1
                    more = b > 0 if right else b < B - 1

                    @pl.when((t < B) if right else (t >= 0))
                    def _(d=d, t=t, slot=slot, to=to, more=more, dist=dist):
                        cp = rdma(inb.at[d, slot], inb.at[d, slot],
                                  i_send.at[d, slot], i_recv.at[d, slot], {"col": to})
                        action(cp, d, t, slot, more, dist < B - 1)

    def inner_send(cp, d, t, slot, more, can):
        if can:
            @pl.when(more)
            def _():
                cp.wait_recv()
                for u in range(tpp):
                    inb[d, slot, part(u)] = inb[d, slot, part(u)] + own(d, t, u)

            @pl.when(jnp.logical_not(more))
            def _():
                for u in range(tpp):
                    inb[d, slot, part(u)] = own(d, t, u)
        else:
            for u in range(tpp):
                inb[d, slot, part(u)] = own(d, t, u)
        cp.start()

    inner_steps(inner_send)

    near = jnp.where(b > 0, b + 1, 0)

    def inner_done(d):
        if B > 1:
            for cond, slot in ((b > 0, b + 1), (b < B - 1, b)):
                @pl.when(cond)
                def _(slot=slot):
                    rdma(inb.at[d, slot], inb.at[d, slot], i_send.at[d, slot],
                         i_recv.at[d, slot], {"row": mate}).wait_recv()
        if B > 2:
            @pl.when((b > 0) & (b < B - 1))
            def _():
                for u in range(tpp):
                    inb[d, b + 1, part(u)] = inb[d, b + 1, part(u)] + inb[d, b, part(u)]

    def here(d, u):
        v = own(d, b, u)
        if B > 1:
            v = v + inb[d, near, part(u)]
        return v

    def outer_copy(s):
        d = pick(s)
        right = d > a
        slot = jnp.where(right, d + 1, d)
        to = jnp.where(right, me_col + B, me_col - B)
        cp = rdma(outb.at[slot], outb.at[slot], o_send.at[slot], o_recv.at[slot], {"col": to})
        return d, right, slot, cp

    for s in range(A - 1):
        d, right, slot, cp = outer_copy(s)
        inner_done(d)
        more = (right & (a > 0)) | (jnp.logical_not(right) & (a < A - 1))

        @pl.when(more)
        def _(d=d, slot=slot, cp=cp):
            cp.wait_recv()
            for u in range(tpp):
                outb[slot, part(u)] = outb[slot, part(u)] + here(d, u)

        @pl.when(jnp.logical_not(more))
        def _(d=d, slot=slot):
            for u in range(tpp):
                outb[slot, part(u)] = here(d, u)

        cp.start()

    inner_done(a)
    for u in range(tpp):
        out_ref[part(u), :] = here(a, u)
    if A > 1:
        for cond, slot in ((a > 0, a + 1), (a < A - 1, a)):
            @pl.when(cond)
            def _(slot=slot):
                rdma(outb.at[slot], outb.at[slot], o_send.at[slot],
                     o_recv.at[slot], {"row": mate}).wait_recv()
                for u in range(tpp):
                    out_ref[part(u), :] = out_ref[part(u), :] + outb[slot, part(u)]
    out_first = (me_row * C + me_col) * (piece // lanes)
    for q in range(piece // lanes):
        at = pl.ds(q * lanes, lanes)
        out_ref[at, :] = out_ref[at, :] * factors(out_first + q)

    for group in (directs.values(), mates, forwards.values()):
        for cp in group:
            cp.wait_send()
    inner_steps(lambda cp, *rest: cp.wait_send())
    for s in range(A - 1):
        outer_copy(s)[-1].wait_send()


def sorted_table(count):
    return [sorted(range(count), key=lambda d: (-abs(d - i), -d)) for i in range(count)]


def body(vectors, tile_values, tile_rows, tile_cols, tile_count, degrees):
    R = lax.axis_size("row")
    C = lax.axis_size("col")
    piece, width = vectors.shape
    side = tile_values.shape[-1]
    slots = tile_values.shape[2]
    B = inner_size(C)
    A = C // B
    tpp = piece // side
    chips = R // 2
    dims = (R, A, B, piece, width, side, slots)
    vmem = pl.BlockSpec(memory_space=pltpu.VMEM)
    smem = pl.BlockSpec(memory_space=pltpu.SMEM)
    dma = pltpu.SemaphoreType.DMA
    f32 = jnp.float32
    far = max(chips - 1, 1)
    return pl.pallas_call(
        functools.partial(kernel, dims),
        out_shape=jax.ShapeDtypeStruct((piece, width), f32),
        in_specs=[smem, smem, smem, vmem, vmem, pl.BlockSpec(memory_space=pl.ANY)],
        out_specs=vmem,
        scratch_shapes=[
            pltpu.VMEM((slots, side, side), tile_values.dtype),
            pltpu.VMEM((R, piece, width), f32),
            pltpu.VMEM((R * tpp, side, 2 * width), jnp.bfloat16),
            pltpu.VMEM((slots + 1, side, width), f32),
            pltpu.VMEM((A, B + 1, piece, width), f32),
            pltpu.VMEM((A + 1, piece, width), f32),
            pltpu.SMEM((slots,), jnp.int32),
            pltpu.SMEM((C * tpp,), jnp.int32),
            dma,
            dma((far, tpp)), dma((far, tpp)),
            dma((tpp,)), dma((tpp,)),
            dma((far, tpp)), dma((far, tpp)),
            dma((A, B + 1)), dma((A, B + 1)),
            dma((A + 1,)), dma((A + 1,)),
        ],
        compiler_params=pltpu.CompilerParams(
            collective_id=0, has_side_effects=True, vmem_limit_bytes=67043328
        ),
    )(tile_rows, tile_cols, tile_count, vectors, degrees.reshape(-1, 128), tile_values)


def solution(mesh):
    placed = (
        P(("col", "row"), None),
        P("row", "col", None, None, None),
        P("row", "col", None),
        P("row", "col", None),
        P("row", "col"),
        P(),
    )
    return jax.shard_map(
        body, mesh=mesh, in_specs=placed, out_specs=P(("row", "col"), None), check_vma=False
    )
```

time: 183 us -> 82.8 us (0.45)
  waiting for transfers between devices: 113 us -> 0 us
  Pallas kernels: 0 us -> 80.1 us
  matrix products: 31.3 us -> 0 us
  local copies, waits for them, and re-layouts: 19 us -> 1.87 us
  between operations: 14.1 us -> 0.66 us
  other arithmetic: 5.01 us -> 0 us
    reduce_scatter x1 -> x0, waiting for transfers between devices: 88.5 us -> none  [body(): lax.psum_scatter(partial_value, 'col', scatter_dimension=0, tiled=True)]
    pallas_call x0 -> x1, Pallas kernels: none -> 80.1 us  [body(): pl.pallas_call(functools.partial(kernel, dims), out_shape=jax.ShapeDtypeS...]
    dot_general x3 -> x0, matrix products: 31.3 us -> none  [the longest x1 20.3 us: body(): jnp.einsum('kij,kjv->kiv', tile_values[0, 0], chosen, precision=lax.Preci...]
    all_gather x1 -> x0, waiting for transfers between devices: 24.7 us -> none  [body(): gathered = lax.all_gather(own_piece, 'row', axis=0, tiled=True)]
    dot_general x1 -> x0, local copies, waits for them, and re-layouts: 6.26 us -> none  [body(): jnp.einsum('kij,kjv->kiv', tile_values[0, 0], chosen, precision=lax.Preci...]
    reshape x2 -> x0, local copies, waits for them, and re-layouts: 5.8 us -> none  [the longest x1 3.83 us: body(): partial_value = partial_value.reshape(row_tiles * tile_side, vec_width)]
    unnamed x4 -> x1, local copies, waits for them, and re-layouts: 6.95 us -> 1.87 us
    mul x2 -> x0, other arithmetic: 4.07 us -> none  [the longest x1 2.04 us: body(): own_piece = vectors * own_scale[:, None]]
  transfers between devices with their start and end apart: 2 -> 0, of which waited for: 2 -> 0; matrix products, arithmetic and copies ran while one was open for 0% -> 0% of each run, Pallas kernels for 0% -> 0%
where the time goes in v1:
time: 82.8 us; the launch traced here: 82.6 us
  Pallas kernels  80.1 us (97%)
  local copies, waits for them, and re-layouts  1.87 us (2%)
    pallas_call x1, Pallas kernels, body(): pl.pallas_call(functools.partial(kernel, dims), out_shape=jax.ShapeDtypeS...  80.1 us
    unnamed x1, local copies, waits for them, and re-layouts  1.87 us

profile of v1, /device:TPU:0, one launch (start us, length us, event | category | flops | bytes accessed | tf_op | source)
XLA Modules:
  0.0 82.6 jit_solution(4211253425814462767)
XLA Ops:
  0.7 80.1 %shard_map.64 = f32[1024,128]{1,0:T(8,128)} custom-call(s32[1,1,22]{2,1,0:T(1,128)} %rows_s.1, s32[1,1,22]{2,1,0:T(1,128)} %cols_s.1, s32[1,1]{1,0:T(1,128)S(6)} %copy.8.count_s, f32[1024,128]{1,0:T(8,128)} %vec_ref.1, s32[256,128]{1,0:T(8,128)} %bitcast.1, bf16[1,1,22,512,512]{4,3,2,1,0:T(8,128)(2,1)} %tiles_hbm.1), custom_call_target="tpu_custom_call" | custom-call | tf_op jit(solution)/shard_map/pallas_call | solution.py:296
  80.7 1.9 %copy.9 = f32[1024,128]{1,0:T(8,128)} copy(f32[1024,128]{1,0:T(8,128)} %shard_map.64) | data formatting | bytes 1048576

commit v2 on v1

--- a/solution.py
+++ b/solution.py
@@ -20,9 +20,9 @@
 def kernel(
     dims,
     rows_s, cols_s, count_s, vec_ref, deg_ref, tiles_hbm, out_ref,
-    tiles_v, gath, split_v, sums, inb, outb, prev_s, last_s,
+    tiles_v, gath, split_v, sums, inb, outb, zb, yb, prev_s, last_s,
     tile_sem, d_send, d_recv, m_send, m_recv, f_send, f_recv,
-    i_send, i_recv, o_send, o_recv,
+    i_send, i_recv, o_send, o_recv, z_send, z_recv, y_send, y_recv,
 ):
     R, A, B, piece, width, side, slots = dims
     C = A * B
@@ -157,6 +157,10 @@
     lax.fori_loop(0, slots, product, 0)
 
     order = sorted_table(A)
+    cut = side - zb.shape[2]
+    head = [(u, u * side, 0, side if u < tpp - 1 else cut) for u in range(tpp)]
+    tail = (tpp - 1) * side + cut
+    tail_rows = side - cut
 
     def pick(s):
         v = jnp.int32(order[0][s])
@@ -164,63 +168,77 @@
             v = jnp.where(a == i, order[i][s], v)
         return v
 
-    def own(d, t, u):
-        return sums[last_s[(d * B + t) * tpp + u]]
-
-    def inner_steps(action):
-        for s in range(A):
-            d = pick(s)
-            for dist in range(B - 1, 0, -1):
-                for right in (True, False):
-                    t = b + dist if right else b - dist
-                    slot = t + 1 if right else t
-                    to = me_col + 1 if right else me_col - 1
-                    more = b > 0 if right else b < B - 1
-
-                    @pl.when((t < B) if right else (t >= 0))
-                    def _(d=d, t=t, slot=slot, to=to, more=more, dist=dist):
-                        cp = rdma(inb.at[d, slot], inb.at[d, slot],
-                                  i_send.at[d, slot], i_recv.at[d, slot], {"col": to})
-                        action(cp, d, t, slot, more, dist < B - 1)
-
-    def inner_send(cp, d, t, slot, more, can):
+    def own(d, t, u, n):
+        return sums[last_s[(d * B + t) * tpp + u], :n]
+
+    def own_tail(d, t):
+        return sums[last_s[(d * B + t) * tpp + tpp - 1], cut:]
+
+    def line(pos, size, stride, dist, action):
+        for right in (True, False):
+            t = pos + dist if right else pos - dist
+            slot = t + 1 if right else t
+            to = me_col + stride if right else me_col - stride
+            more = pos > 0 if right else pos < size - 1
+
+            @pl.when((t < size) if right else (t >= 0))
+            def _(t=t, slot=slot, to=to, more=more):
+                action(t, slot, to, more, dist < size - 1)
+
+    def add_and_send(cp, more, can, store):
         if can:
             @pl.when(more)
             def _():
                 cp.wait_recv()
-                for u in range(tpp):
-                    inb[d, slot, part(u)] = inb[d, slot, part(u)] + own(d, t, u)
+                store(True)
 
             @pl.when(jnp.logical_not(more))
             def _():
-                for u in range(tpp):
-                    inb[d, slot, part(u)] = own(d, t, u)
+                store(False)
         else:
-            for u in range(tpp):
-                inb[d, slot, part(u)] = own(d, t, u)
+            store(False)
         cp.start()
 
-    inner_steps(inner_send)
-
-    near = jnp.where(b > 0, b + 1, 0)
-
-    def inner_done(d):
-        if B > 1:
-            for cond, slot in ((b > 0, b + 1), (b < B - 1, b)):
+    def arrive(pos, size, ref, ssem, rsem, fold):
+        if size > 1:
+            for cond, slot in ((pos > 0, pos + 1), (pos < size - 1, pos)):
                 @pl.when(cond)
                 def _(slot=slot):
-                    rdma(inb.at[d, slot], inb.at[d, slot], i_send.at[d, slot],
-                         i_recv.at[d, slot], {"row": mate}).wait_recv()
-        if B > 2:
-            @pl.when((b > 0) & (b < B - 1))
+                    rdma(ref(slot), ref(slot), ssem(slot), rsem(slot), {"row": mate}).wait_recv()
+        if size > 2:
+            @pl.when((pos > 0) & (pos < size - 1))
             def _():
-                for u in range(tpp):
-                    inb[d, b + 1, part(u)] = inb[d, b + 1, part(u)] + inb[d, b, part(u)]
-
-    def here(d, u):
-        v = own(d, b, u)
+                fold(pos + 1, pos)
+
+    near = jnp.where(b > 0, b + 1, 0)
+    near_a = jnp.where(a > 0, a + 1, 0)
+
+    def inner_copy(d, slot, to):
+        at = inb.at[d, slot]
+        return rdma(at, at, i_send.at[d, slot], i_recv.at[d, slot], {"col": to})
+
+    def inner_send(d):
+        def action(t, slot, to, more, can):
+            def store(add):
+                for u, at, _, n in head:
+                    rows = pl.ds(at, n)
+                    v = own(d, t, u, n)
+                    inb[d, slot, rows] = inb[d, slot, rows] + v if add else v
+
+            add_and_send(inner_copy(d, slot, to), more, can, store)
+        return action
+
+    def inner_done(d):
+        def fold(x, y):
+            inb[d, x] = inb[d, x] + inb[d, y]
+
+        arrive(b, B, lambda q: inb.at[d, q], lambda q: i_send.at[d, q],
+               lambda q: i_recv.at[d, q], fold)
+
+    def here(d, u, at, n):
+        v = own(d, b, u, n)
         if B > 1:
-            v = v + inb[d, near, part(u)]
+            v = v + inb[d, near, pl.ds(at, n)]
         return v
 
     def outer_copy(s):
@@ -231,35 +249,89 @@
         cp = rdma(outb.at[slot], outb.at[slot], o_send.at[slot], o_recv.at[slot], {"col": to})
         return d, right, slot, cp
 
-    for s in range(A - 1):
+    def outer_step(s):
         d, right, slot, cp = outer_copy(s)
         inner_done(d)
         more = (right & (a > 0)) | (jnp.logical_not(right) & (a < A - 1))
 
-        @pl.when(more)
-        def _(d=d, slot=slot, cp=cp):
-            cp.wait_recv()
-            for u in range(tpp):
-                outb[slot, part(u)] = outb[slot, part(u)] + here(d, u)
-
-        @pl.when(jnp.logical_not(more))
-        def _(d=d, slot=slot):
-            for u in range(tpp):
-                outb[slot, part(u)] = here(d, u)
-
-        cp.start()
+        def store(add):
+            for u, at, _, n in head:
+                rows = pl.ds(at, n)
+                v = here(d, u, at, n)
+                outb[slot, rows] = outb[slot, rows] + v if add else v
+
+        add_and_send(cp, more, True, store)
+
+    def zcopy(slot, to):
+        return rdma(zb.at[slot], zb.at[slot], z_send.at[slot], z_recv.at[slot], {"col": to})
+
+    def zsend(d, slot, to, more, can):
+        def store(add):
+            for t in range(B):
+                v = own_tail(d, t)
+                zb[slot, t] = zb[slot, t] + v if add else v
+
+        add_and_send(zcopy(slot, to), more, can, store)
+
+    def zhere(t):
+        v = own_tail(a, t)
+        if A > 1:
+            v = v + zb[near_a, t]
+        return v
+
+    def ycopy(slot, to):
+        return rdma(yb.at[slot], yb.at[slot], y_send.at[slot], y_recv.at[slot], {"col": to})
+
+    def ysend(t, slot, to, more, can):
+        def store(add):
+            v = zhere(t)
+            yb[slot] = yb[slot] + v if add else v
+
+        add_and_send(ycopy(slot, to), more, can, store)
+
+    def zfold(x, y):
+        zb[x] = zb[x] + zb[y]
+
+    def yfold(x, y):
+        yb[x] = yb[x] + yb[y]
+
+    def tail_turn():
+        arrive(a, A, lambda q: zb.at[q], lambda q: z_send.at[q], lambda q: z_recv.at[q], zfold)
+        for dist in range(B - 1, 0, -1):
+            line(b, B, 1, dist, ysend)
+
+    if A > 1:
+        line(a, A, B, A - 1, zsend)
+    for s in range(A):
+        for dist in range(B - 1, 0, -1):
+            line(b, B, 1, dist, inner_send(pick(s)))
+    for dist in range(A - 2, 1, -1):
+        line(a, A, B, dist, zsend)
+    turn = min(1, A - 2)
+    for s in range(A - 1):
+        outer_step(s)
+        if s == 0 and A > 2:
+            line(a, A, B, 1, zsend)
+        if s == turn:
+            tail_turn()
+    if A == 1:
+        tail_turn()
 
     inner_done(a)
-    for u in range(tpp):
-        out_ref[part(u), :] = here(a, u)
+    for u, at, _, n in head:
+        out_ref[pl.ds(at, n), :] = here(a, u, at, n)
     if A > 1:
         for cond, slot in ((a > 0, a + 1), (a < A - 1, a)):
             @pl.when(cond)
             def _(slot=slot):
                 rdma(outb.at[slot], outb.at[slot], o_send.at[slot],
                      o_recv.at[slot], {"row": mate}).wait_recv()
-                for u in range(tpp):
-                    out_ref[part(u), :] = out_ref[part(u), :] + outb[slot, part(u)]
+                out_ref[pl.ds(0, tail), :] = out_ref[pl.ds(0, tail), :] + outb[slot]
+    arrive(b, B, lambda q: yb.at[q], lambda q: y_send.at[q], lambda q: y_recv.at[q], yfold)
+    last = zhere(b)
+    if B > 1:
+        last = last + yb[near]
+    out_ref[pl.ds(tail, tail_rows), :] = last
     out_first = (me_row * C + me_col) * (piece // lanes)
     for q in range(piece // lanes):
         at = pl.ds(q * lanes, lanes)
@@ -268,7 +340,13 @@
     for group in (directs.values(), mates, forwards.values()):
         for cp in group:
             cp.wait_send()
-    inner_steps(lambda cp, *rest: cp.wait_send())
+    for dist in range(A - 1, 0, -1):
+        line(a, A, B, dist, lambda t, slot, to, *rest: zcopy(slot, to).wait_send())
+    for dist in range(B - 1, 0, -1):
+        line(b, B, 1, dist, lambda t, slot, to, *rest: ycopy(slot, to).wait_send())
+        for s in range(A):
+            d = pick(s)
+            line(b, B, 1, dist, lambda t, slot, to, *rest, d=d: inner_copy(d, slot, to).wait_send())
     for s in range(A - 1):
         outer_copy(s)[-1].wait_send()
 
@@ -293,6 +371,7 @@
     dma = pltpu.SemaphoreType.DMA
     f32 = jnp.float32
     far = max(chips - 1, 1)
+    tail_rows = -(-piece // 96) * 16
     return pl.pallas_call(
         functools.partial(kernel, dims),
         out_shape=jax.ShapeDtypeStruct((piece, width), f32),
@@ -303,8 +382,10 @@
             pltpu.VMEM((R, piece, width), f32),
             pltpu.VMEM((R * tpp, side, 2 * width), jnp.bfloat16),
             pltpu.VMEM((slots + 1, side, width), f32),
-            pltpu.VMEM((A, B + 1, piece, width), f32),
-            pltpu.VMEM((A + 1, piece, width), f32),
+            pltpu.VMEM((A, B + 1, piece - tail_rows, width), f32),
+            pltpu.VMEM((A + 1, piece - tail_rows, width), f32),
+            pltpu.VMEM((A + 1, B, tail_rows, width), f32),
+            pltpu.VMEM((B + 1, tail_rows, width), f32),
             pltpu.SMEM((slots,), jnp.int32),
             pltpu.SMEM((C * tpp,), jnp.int32),
             dma,
@@ -313,6 +394,8 @@
             dma((far, tpp)), dma((far, tpp)),
             dma((A, B + 1)), dma((A, B + 1)),
             dma((A + 1,)), dma((A + 1,)),
+            dma((A + 1,)), dma((A + 1,)),
+            dma((B + 1,)), dma((B + 1,)),
         ],
         compiler_params=pltpu.CompilerParams(
             collective_id=0, has_side_effects=True, vmem_limit_bytes=67043328

time: 82.8 us -> 78.3 us (0.946)
  Pallas kernels: 80.1 us -> 75.6 us
    pallas_call x1, Pallas kernels: 80.1 us -> 75.6 us  [body(): pl.pallas_call(functools.partial(kernel, dims), out_shape=jax.ShapeDtypeS...]
where the time goes in v2:
time: 78.3 us; the launch traced here: 78.1 us
  Pallas kernels  75.6 us (97%)
  local copies, waits for them, and re-layouts  1.87 us (2%)
    pallas_call x1, Pallas kernels, body(): pl.pallas_call(functools.partial(kernel, dims), out_shape=jax.ShapeDtypeS...  75.6 us
    unnamed x1, local copies, waits for them, and re-layouts  1.87 us

profile of v2, /device:TPU:0, one launch (start us, length us, event | category | flops | bytes accessed | tf_op | source)
XLA Modules:
  0.0 78.1 jit_solution(843687653074258347)
XLA Ops:
  0.7 75.6 %shard_map.64 = f32[1024,128]{1,0:T(8,128)} custom-call(s32[1,1,22]{2,1,0:T(1,128)} %rows_s.1, s32[1,1,22]{2,1,0:T(1,128)} %cols_s.1, s32[1,1]{1,0:T(1,128)S(6)} %copy.8.count_s, f32[1024,128]{1,0:T(8,128)} %vec_ref.1, s32[256,128]{1,0:T(8,128)} %bitcast.1, bf16[1,1,22,512,512]{4,3,2,1,0:T(8,128)(2,1)} %tiles_hbm.1), custom_call_target="tpu_custom_call" | custom-call | tf_op jit(solution)/shard_map/pallas_call | solution.py:375
  76.3 1.9 %copy.9 = f32[1024,128]{1,0:T(8,128)} copy(f32[1024,128]{1,0:T(8,128)} %shard_map.64) | data formatting | bytes 1048576

commit v3 on v2

--- a/solution.py
+++ b/solution.py
@@ -21,7 +21,7 @@
     dims,
     rows_s, cols_s, count_s, vec_ref, deg_ref, tiles_hbm, out_ref,
     tiles_v, gath, split_v, sums, inb, outb, zb, yb, prev_s, last_s,
-    tile_sem, d_send, d_recv, m_send, m_recv, f_send, f_recv,
+    tile_sem, vec_sem, d_send, d_recv, m_send, m_recv, f_send, f_recv,
     i_send, i_recv, o_send, o_recv, z_send, z_recv, y_send, y_recv,
 ):
     R, A, B, piece, width, side, slots = dims
@@ -83,6 +83,9 @@
         cp.start()
         mates.append(cp)
 
+    vec_copy = pltpu.make_async_copy(vec_ref, gath.at[me_row], vec_sem)
+    vec_copy.start()
+
     count = count_s[0, 0]
 
     def link(k, _):
@@ -127,8 +130,9 @@
     def landed(r, c, ssem, rsem):
         rdma(gath.at[r, part(c)], gath.at[r, part(c)], ssem, rsem, {"row": mate}).wait_recv()
 
-    for c in range(tpp):
-        scale(lambda s: vec_ref[s, :], me_row, c)
+    vec_copy.wait()
+    for c in range(tpp):
+        scale(lambda s: gath[me_row, s, :], me_row, c)
     for c in range(tpp):
         landed(mate, c, m_send.at[c], m_recv.at[c])
         scale(lambda s: gath[mate, s, :], mate, c)
@@ -149,18 +153,26 @@
 
     tile_copy.wait()
 
-    def product(k, _):
-        both = jnp.dot(tiles_v[k], split_v[cols_s[0, 0, k]], preferred_element_type=jnp.float32)
-        sums[k] = both[:, :width] + both[:, width:] + sums[prev_s[k]]
-        return 0
-
-    lax.fori_loop(0, slots, product, 0)
+    def products(lo, n):
+        def product(k, _):
+            both = jnp.dot(tiles_v[k, lo:lo + n], split_v[cols_s[0, 0, k]],
+                           preferred_element_type=jnp.float32)
+            old = sums[prev_s[k], lo:lo + n]
+            sums[k, lo:lo + n] = both[:, :width] + both[:, width:] + old
+            return 0
+
+        lax.fori_loop(0, slots, product, 0)
 
     order = sorted_table(A)
     cut = side - zb.shape[2]
-    head = [(u, u * side, 0, side if u < tpp - 1 else cut) for u in range(tpp)]
     tail = (tpp - 1) * side + cut
     tail_rows = side - cut
+    early = [(u, u * tail_rows, cut, tail_rows) for u in range(tpp - 1)]
+    late_at = (tpp - 1) * tail_rows
+    late = [(u, late_at + u * cut, 0, cut) for u in range(tpp)]
+    spans = [(late_at, tpp * cut, late)]
+    if early:
+        spans = [(0, late_at, early)] + spans
 
     def pick(s):
         v = jnp.int32(order[0][s])
@@ -168,8 +180,8 @@
             v = jnp.where(a == i, order[i][s], v)
         return v
 
-    def own(d, t, u, n):
-        return sums[last_s[(d * B + t) * tpp + u], :n]
+    def own(d, t, u, lo, n):
+        return sums[last_s[(d * B + t) * tpp + u], lo:lo + n]
 
     def own_tail(d, t):
         return sums[last_s[(d * B + t) * tpp + tpp - 1], cut:]
@@ -213,51 +225,53 @@
     near = jnp.where(b > 0, b + 1, 0)
     near_a = jnp.where(a > 0, a + 1, 0)
 
-    def inner_copy(d, slot, to):
-        at = inb.at[d, slot]
-        return rdma(at, at, i_send.at[d, slot], i_recv.at[d, slot], {"col": to})
-
-    def inner_send(d):
+    def inner_copy(h, d, slot, to):
+        at = inb.at[d, slot, pl.ds(*spans[h][:2])]
+        return rdma(at, at, i_send.at[h, d, slot], i_recv.at[h, d, slot], {"col": to})
+
+    def inner_send(h, d):
         def action(t, slot, to, more, can):
             def store(add):
-                for u, at, _, n in head:
+                for u, at, lo, n in spans[h][2]:
                     rows = pl.ds(at, n)
-                    v = own(d, t, u, n)
+                    v = own(d, t, u, lo, n)
                     inb[d, slot, rows] = inb[d, slot, rows] + v if add else v
 
-            add_and_send(inner_copy(d, slot, to), more, can, store)
+            add_and_send(inner_copy(h, d, slot, to), more, can, store)
         return action
 
-    def inner_done(d):
+    def inner_done(h, d):
+        rows = pl.ds(*spans[h][:2])
+
         def fold(x, y):
-            inb[d, x] = inb[d, x] + inb[d, y]
-
-        arrive(b, B, lambda q: inb.at[d, q], lambda q: i_send.at[d, q],
-               lambda q: i_recv.at[d, q], fold)
-
-    def here(d, u, at, n):
-        v = own(d, b, u, n)
+            inb[d, x, rows] = inb[d, x, rows] + inb[d, y, rows]
+
+        arrive(b, B, lambda q: inb.at[d, q, rows], lambda q: i_send.at[h, d, q],
+               lambda q: i_recv.at[h, d, q], fold)
+
+    def here(d, u, at, lo, n):
+        v = own(d, b, u, lo, n)
         if B > 1:
             v = v + inb[d, near, pl.ds(at, n)]
         return v
 
-    def outer_copy(s):
+    def outer_copy(h, s):
         d = pick(s)
         right = d > a
         slot = jnp.where(right, d + 1, d)
         to = jnp.where(right, me_col + B, me_col - B)
-        cp = rdma(outb.at[slot], outb.at[slot], o_send.at[slot], o_recv.at[slot], {"col": to})
-        return d, right, slot, cp
-
-    def outer_step(s):
-        d, right, slot, cp = outer_copy(s)
-        inner_done(d)
+        at = outb.at[slot, pl.ds(*spans[h][:2])]
+        return d, right, slot, rdma(at, at, o_send.at[h, slot], o_recv.at[h, slot], {"col": to})
+
+    def outer_step(h, s):
+        d, right, slot, cp = outer_copy(h, s)
+        inner_done(h, d)
         more = (right & (a > 0)) | (jnp.logical_not(right) & (a < A - 1))
 
         def store(add):
-            for u, at, _, n in head:
+            for u, at, lo, n in spans[h][2]:
                 rows = pl.ds(at, n)
-                v = here(d, u, at, n)
+                v = here(d, u, at, lo, n)
                 outb[slot, rows] = outb[slot, rows] + v if add else v
 
         add_and_send(cp, more, True, store)
@@ -300,33 +314,51 @@
         for dist in range(B - 1, 0, -1):
             line(b, B, 1, dist, ysend)
 
+    def inner_all(h):
+        for s in range(A):
+            for dist in range(B - 1, 0, -1):
+                line(b, B, 1, dist, inner_send(h, pick(s)))
+
+    products(cut, tail_rows)
     if A > 1:
         line(a, A, B, A - 1, zsend)
-    for s in range(A):
-        for dist in range(B - 1, 0, -1):
-            line(b, B, 1, dist, inner_send(pick(s)))
+    if early:
+        inner_all(0)
+    products(0, cut)
+    inner_all(len(spans) - 1)
     for dist in range(A - 2, 1, -1):
         line(a, A, B, dist, zsend)
-    turn = min(1, A - 2)
-    for s in range(A - 1):
-        outer_step(s)
-        if s == 0 and A > 2:
-            line(a, A, B, 1, zsend)
-        if s == turn:
-            tail_turn()
+    turn = (len(spans) - 1, 0)
+    for h in range(len(spans)):
+        for s in range(A - 1):
+            outer_step(h, s)
+            if (h, s) == (0, 0) and A > 2:
+                line(a, A, B, 1, zsend)
+            if (h, s) == turn:
+                tail_turn()
     if A == 1:
         tail_turn()
 
-    inner_done(a)
-    for u, at, _, n in head:
-        out_ref[pl.ds(at, n), :] = here(a, u, at, n)
-    if A > 1:
-        for cond, slot in ((a > 0, a + 1), (a < A - 1, a)):
-            @pl.when(cond)
-            def _(slot=slot):
-                rdma(outb.at[slot], outb.at[slot], o_send.at[slot],
-                     o_recv.at[slot], {"row": mate}).wait_recv()
-                out_ref[pl.ds(0, tail), :] = out_ref[pl.ds(0, tail), :] + outb[slot]
+    for h in range(len(spans)):
+        inner_done(h, a)
+        first, rows, parts = spans[h]
+        if A > 1:
+            for cond, slot in ((a > 0, a + 1), (a < A - 1, a)):
+                @pl.when(cond)
+                def _(slot=slot, h=h, first=first, rows=rows):
+                    at = outb.at[slot, pl.ds(first, rows)]
+                    rdma(at, at, o_send.at[h, slot], o_recv.at[h, slot],
+                         {"row": mate}).wait_recv()
+        if A > 2:
+            @pl.when((a > 0) & (a < A - 1))
+            def _(first=first, rows=rows):
+                at = pl.ds(first, rows)
+                outb[a + 1, at] = outb[a + 1, at] + outb[a, at]
+        for u, at, lo, n in parts:
+            v = here(a, u, at, lo, n)
+            if A > 1:
+                v = v + outb[near_a, pl.ds(at, n)]
+            out_ref[pl.ds(u * side + lo, n), :] = v
     arrive(b, B, lambda q: yb.at[q], lambda q: y_send.at[q], lambda q: y_recv.at[q], yfold)
     last = zhere(b)
     if B > 1:
@@ -344,11 +376,15 @@
         line(a, A, B, dist, lambda t, slot, to, *rest: zcopy(slot, to).wait_send())
     for dist in range(B - 1, 0, -1):
         line(b, B, 1, dist, lambda t, slot, to, *rest: ycopy(slot, to).wait_send())
-        for s in range(A):
-            d = pick(s)
-            line(b, B, 1, dist, lambda t, slot, to, *rest, d=d: inner_copy(d, slot, to).wait_send())
-    for s in range(A - 1):
-        outer_copy(s)[-1].wait_send()
+        for h in range(len(spans)):
+            for s in range(A):
+                def left(t, slot, to, *rest, h=h, d=pick(s)):
+                    inner_copy(h, d, slot, to).wait_send()
+
+                line(b, B, 1, dist, left)
+    for h in range(len(spans)):
+        for s in range(A - 1):
+            outer_copy(h, s)[-1].wait_send()
 
 
 def sorted_table(count):
@@ -375,7 +411,7 @@
     return pl.pallas_call(
         functools.partial(kernel, dims),
         out_shape=jax.ShapeDtypeStruct((piece, width), f32),
-        in_specs=[smem, smem, smem, vmem, vmem, pl.BlockSpec(memory_space=pl.ANY)],
+        in_specs=[smem, smem, smem, pl.BlockSpec(memory_space=pl.ANY), vmem, pl.BlockSpec(memory_space=pl.ANY)],
         out_specs=vmem,
         scratch_shapes=[
             pltpu.VMEM((slots, side, side), tile_values.dtype),
@@ -388,12 +424,12 @@
             pltpu.VMEM((B + 1, tail_rows, width), f32),
             pltpu.SMEM((slots,), jnp.int32),
             pltpu.SMEM((C * tpp,), jnp.int32),
-            dma,
+            dma, dma,
             dma((far, tpp)), dma((far, tpp)),
             dma((tpp,)), dma((tpp,)),
             dma((far, tpp)), dma((far, tpp)),
-            dma((A, B + 1)), dma((A, B + 1)),
-            dma((A + 1,)), dma((A + 1,)),
+            dma((2, A, B + 1)), dma((2, A, B + 1)),
+            dma((2, A + 1)), dma((2, A + 1)),
             dma((A + 1,)), dma((A + 1,)),
             dma((B + 1,)), dma((B + 1,)),
         ],

time: 78.3 us -> 77 us (0.983)
  Pallas kernels: 75.6 us -> 74.3 us
    pallas_call x1, Pallas kernels: 75.6 us -> 74.3 us  [body(): pl.pallas_call(functools.partial(kernel, dims), out_shape=jax.ShapeDtypeS...]
where the time goes in v3:
time: 77 us; the launch traced here: 76.8 us
  Pallas kernels  74.3 us (96%)
  local copies, waits for them, and re-layouts  1.87 us (2%)
    pallas_call x1, Pallas kernels, body(): pl.pallas_call(functools.partial(kernel, dims), out_shape=jax.ShapeDtypeS...  74.3 us
    unnamed x1, local copies, waits for them, and re-layouts  1.87 us

profile of v3, /device:TPU:0, one launch (start us, length us, event | category | flops | bytes accessed | tf_op | source)
XLA Modules:
  0.0 76.8 jit_solution(14500606183654654814)
XLA Ops:
  0.7 74.3 %shard_map.64 = f32[1024,128]{1,0:T(8,128)} custom-call(s32[1,1,22]{2,1,0:T(1,128)} %rows_s.1, s32[1,1,22]{2,1,0:T(1,128)} %cols_s.1, s32[1,1]{1,0:T(1,128)S(6)} %copy.8.count_s, f32[1024,128]{1,0:T(8,128)} %vec_ref.1, s32[256,128]{1,0:T(8,128)} %bitcast.1, bf16[1,1,22,512,512]{4,3,2,1,0:T(8,128)(2,1)} %tiles_hbm.1), custom_call_target="tpu_custom_call" | custom-call | tf_op jit(solution)/shard_map/pallas_call | solution.py:411
  75.0 1.9 %copy.9 = f32[1024,128]{1,0:T(8,128)} copy(f32[1024,128]{1,0:T(8,128)} %shard_map.64) | data formatting | bytes 1048576

commit v4 on v3

--- a/solution.py
+++ b/solution.py
@@ -161,7 +161,7 @@
             sums[k, lo:lo + n] = both[:, :width] + both[:, width:] + old
             return 0
 
-        lax.fori_loop(0, slots, product, 0)
+        lax.fori_loop(0, slots, product, 0, unroll=True)
 
     order = sorted_table(A)
     cut = side - zb.shape[2]

time: 77 us -> 70.8 us (0.919)
  Pallas kernels: 74.3 us -> 68.1 us
    pallas_call x1, Pallas kernels: 74.3 us -> 68.1 us  [body(): pl.pallas_call(functools.partial(kernel, dims), out_shape=jax.ShapeDtypeS...]
where the time goes in v4:
time: 70.8 us; the launch traced here: 70.7 us
  Pallas kernels  68.1 us (96%)
  local copies, waits for them, and re-layouts  1.87 us (3%)
    pallas_call x1, Pallas kernels, body(): pl.pallas_call(functools.partial(kernel, dims), out_shape=jax.ShapeDtypeS...  68.1 us
    unnamed x1, local copies, waits for them, and re-layouts  1.87 us

profile of v4, /device:TPU:0, one launch (start us, length us, event | category | flops | bytes accessed | tf_op | source)
XLA Modules:
  0.0 70.7 jit_solution(18028429950329175754)
XLA Ops:
  0.7 68.1 %shard_map.64 = f32[1024,128]{1,0:T(8,128)} custom-call(s32[1,1,22]{2,1,0:T(1,128)} %rows_s.1, s32[1,1,22]{2,1,0:T(1,128)} %cols_s.1, s32[1,1]{1,0:T(1,128)S(6)} %copy.8.count_s, f32[1024,128]{1,0:T(8,128)} %vec_ref.1, s32[256,128]{1,0:T(8,128)} %bitcast.1, bf16[1,1,22,512,512]{4,3,2,1,0:T(8,128)(2,1)} %tiles_hbm.1), custom_call_target="tpu_custom_call" | custom-call | tf_op jit(solution)/shard_map/pallas_call | solution.py:411
  68.8 1.9 %copy.9 = f32[1024,128]{1,0:T(8,128)} copy(f32[1024,128]{1,0:T(8,128)} %shard_map.64) | data formatting | bytes 1048576

commit v5 on v4

--- a/solution.py
+++ b/solution.py
@@ -125,7 +125,7 @@
             split_v[r * tpp + c, at, width:] = lo
             return 0
 
-        lax.fori_loop(0, side // lanes, step, 0)
+        lax.fori_loop(0, side // lanes, step, 0, unroll=True)
 
     def landed(r, c, ssem, rsem):
         rdma(gath.at[r, part(c)], gath.at[r, part(c)], ssem, rsem, {"row": mate}).wait_recv()

time: 70.8 us -> 71.3 us (level)
  no operation moved by 1% of the time
where the time goes in v5:
time: 71.3 us; the launch traced here: 71.1 us
  Pallas kernels  68.6 us (96%)
  local copies, waits for them, and re-layouts  1.87 us (3%)
    pallas_call x1, Pallas kernels, body(): pl.pallas_call(functools.partial(kernel, dims), out_shape=jax.ShapeDtypeS...  68.6 us
    unnamed x1, local copies, waits for them, and re-layouts  1.87 us

profile of v5, /device:TPU:0, one launch (start us, length us, event | category | flops | bytes accessed | tf_op | source)
XLA Modules:
  0.0 71.1 jit_solution(14000248642484870330)
XLA Ops:
  0.7 68.6 %shard_map.64 = f32[1024,128]{1,0:T(8,128)} custom-call(s32[1,1,22]{2,1,0:T(1,128)} %rows_s.1, s32[1,1,22]{2,1,0:T(1,128)} %cols_s.1, s32[1,1]{1,0:T(1,128)S(6)} %copy.8.count_s, f32[1024,128]{1,0:T(8,128)} %vec_ref.1, s32[256,128]{1,0:T(8,128)} %bitcast.1, bf16[1,1,22,512,512]{4,3,2,1,0:T(8,128)(2,1)} %tiles_hbm.1), custom_call_target="tpu_custom_call" | custom-call | tf_op jit(solution)/shard_map/pallas_call | solution.py:411
  69.3 1.9 %copy.9 = f32[1024,128]{1,0:T(8,128)} copy(f32[1024,128]{1,0:T(8,128)} %shard_map.64) | data formatting | bytes 1048576
